TPU v7x, 128 devices: a whole 4x4x4 slice. The times are simulated.
128 devices in a mesh: ublk: 16 (over x, z), salt: 8 (over y, core).
Axes of the slice: x: 4, y: 4, z: 4, core: 2. Of those that a mesh axis runs over, the one named last changes fastest.
Arguments:
- user_factors: bfloat16 [16, 8192, 256], P('ublk', 'salt')
- tile_users: int32 [16, 8, 4096], P('ublk', 'salt'), may hold values from 0 to 8191
- tile_items: int32 [16, 8, 4096], P('ublk', 'salt'), may hold values from 0 to 511
- tile_weight: float32 [16, 8, 4096], P('ublk', 'salt'), may hold values from 0.5 to 8
- live_count: int32 [16, 8], P('ublk', 'salt'), may hold values from 2048 to 4096, as said below
Outputs:
- item_factors: float32 [8, 512, 256], P('salt', 'ublk')
- residual: float32 [8, 512, 256], P('salt', 'ublk')
Inputs may be any that keep to these rules, and one draw needn't show every extreme that they name: Every entry of live_count is at least 2048 and at most 4096; some tile is full.
All inputs are finite; a program needn't handle non-finite values.
Results may differ from a plain program's by a relative error of at most 0.0022.
Values may be sent and summed in bfloat16 or wider, within the bound.
A program may use at most 64 MiB of HBM per device.

v0:
```python
import jax
import jax.numpy as jnp
from jax import lax
from jax.sharding import PartitionSpec as P

ITERS = 8
ITEM_DEV = 32
REG = 1.0
EPS = 1e-06


def conjugate(rhs, image_of):
    solution = jnp.zeros_like(rhs)
    resid = rhs
    direction = rhs
    norm_now = jnp.sum(resid * resid, axis=1)
    for step in range(ITERS):
        image = image_of(direction)
        alpha = norm_now / (jnp.sum(direction * image, axis=1) + EPS)
        solution = solution + alpha[:, None] * direction
        resid = resid - alpha[:, None] * image
        norm_next = jnp.sum(resid * resid, axis=1)
        direction = resid + (norm_next / (norm_now + EPS))[:, None] * direction
        norm_now = norm_next
    return (solution, resid)


def body(user_factors, tile_users, tile_items, tile_weight, live_count):
    shard = user_factors[0]
    block = lax.all_gather(shard, "salt", axis=0, tiled=True)
    contract = (((0,), (0,)), ((), ()))
    own_gram = lax.dot_general(shard, shard, contract, preferred_element_type=jnp.float32)
    gram = lax.psum(own_gram, ("ublk", "salt"))
    users = tile_users[0, 0]
    items = tile_items[0, 0]
    raw = tile_weight[0, 0]
    live = jnp.arange(users.shape[0], dtype=jnp.int32) < live_count[0, 0]
    weight = jnp.where(live, raw, jnp.zeros_like(raw))
    confid = jnp.where(live, 1.0 + raw, jnp.zeros_like(raw))
    rows = jnp.take(block, users, axis=0).astype(jnp.float32)
    column_items = ITEM_DEV * lax.axis_size("ublk")
    rhs_terms = jax.ops.segment_sum(confid[:, None] * rows, items, num_segments=column_items)

    def local_terms(whole_dir):
        along = jnp.sum(rows * whole_dir[items], axis=1) * weight
        return jax.ops.segment_sum(along[:, None] * rows, items, num_segments=column_items)

    def finish(summed, direction):
        return summed + jnp.dot(direction, gram, precision=lax.Precision.HIGHEST) + REG * direction

    rhs = lax.psum(rhs_terms, "ublk")

    def image_every(direction):
        summed = lax.psum(local_terms(direction), "ublk")
        return finish(summed, direction)

    solution_all, resid_all = conjugate(rhs, image_every)
    start = lax.axis_index("ublk") * ITEM_DEV
    solution = lax.dynamic_slice_in_dim(solution_all, start, ITEM_DEV, 0)
    resid = lax.dynamic_slice_in_dim(resid_all, start, ITEM_DEV, 0)
    return (solution[None], resid[None])


def solution(mesh):
    return jax.shard_map(
        body,
        mesh=mesh,
        in_specs=(
            P("ublk", "salt", None),
            P("ublk", "salt", None),
            P("ublk", "salt", None),
            P("ublk", "salt", None),
            P("ublk", "salt"),
        ),
        out_specs=(P("salt", "ublk", None), P("salt", "ublk", None)),
        check_vma=False,
    )
```

profile of v0, /device:TPU:0, one launch (start us, length us, event | category | flops | bytes accessed | tf_op | source)
XLA Modules:
  0.0 1352.9 jit_solution(7503660293953594438)
XLA Ops:
  10.8 33.5 %all-gather.3.cloned.1.call-done = bf16[1,8192,256]{2,1,0:T(8,128)(2,1)} async-done(((bf16[1,1024,256]{2,1,0:T(8,128)(2,1)}), bf16[1,8192,256]{2,1,0:T(8,128)(2,1)}) %all-gather.3.cloned.1.call-update) | async-done | bytes 4194320 | tf_op jit(solution)/shard_map/all_gather | solution.py:30
  60.1 26.1 %scatter_custom_fusion = f32[512,256]{1,0:T(8,128)} fusion(s32[4096]{0:T(1024)S(1)} %bitcast.56, f32[4096]{0:T(1024)S(1)} %add_select_fusion, f32[]{:T(128)} %constant.11.clone.1, bf16[4096,256]{1,0:T(8,128)(2,1)S(1)} %gather_fusion, pred[4096]{0:T(1024)(128)(4,1)S(1)} %compare_and_fusion), kind=kCustom, calls=%fused_computation.35 | custom fusion | flops 4194304 | bytes 2641924 | tf_op jit(solution)/shard_map/scatter-add | solution.py:42
  87.4 84.7 %all-reduce.11.cloned.1.call-done = f32[512,256]{1,0:T(8,128)} async-done(((f32[512,256]{1,0:T(8,128)}), f32[512,256]{1,0:T(8,128)}) %all-reduce.11.cloned.1.call-update) | async-done | bytes 524304 | tf_op jit(solution)/shard_map/psum | solution.py:51
  172.1 17.1 %gather_fusion.1 = f32[4096,256]{1,0:T(8,128)} fusion(f32[512,256]{1,0:T(8,128)} %all-reduce.11.cloned.1.call-done, s32[4096]{0:T(1024)S(1)} %broadcast_clamp_fusion), kind=kCustom, calls=%fused_computation.1 | custom fusion | bytes 8404992 | tf_op jit(solution)/shard_map/gather | solution.py:45
  192.2 26.1 %scatter_custom_fusion.1 = f32[512,256]{1,0:T(8,128)} fusion(s32[4096]{0:T(1024)S(1)} %bitcast.57, f32[4096]{0:T(1024)S(1)} %fusion.60, f32[]{:T(128)} %constant.11.clone.1, bf16[4096,256]{1,0:T(8,128)(2,1)S(1)} %gather_fusion, pred[4096]{0:T(1024)(128)(4,1)S(1)} %compare_and_fusion), kind=kCustom, calls=%fused_computation.37 | custom fusion | flops 4194304 | bytes 2641924 | tf_op jit(solution)/shard_map/scatter-add | solution.py:46
  218.7 100.7 %all-reduce.15.cloned.1.call-done = f32[256,256]{1,0:T(8,128)} async-done(((f32[256,256]{1,0:T(8,128)}), f32[256,256]{1,0:T(8,128)}) %all-reduce.15.cloned.1.call-update) | async-done | bytes 262160 | tf_op jit(solution)/shard_map/psum | solution.py:33
  319.4 86.2 %all-reduce.13.cloned.1.call-done = f32[512,256]{1,0:T(8,128)} async-done(((f32[512,256]{1,0:T(8,128)}), f32[512,256]{1,0:T(8,128)}) %all-reduce.13.cloned.1.call-update) | async-done | bytes 524304 | tf_op jit(solution)/shard_map/psum | solution.py:54
  408.4 16.1 %gather_fusion.2 = f32[4096,256]{1,0:T(8,128)} fusion(f32[512,256]{1,0:T(8,128)S(1)} %multiply_add_fusion.7, s32[4096]{0:T(1024)S(1)} %broadcast_clamp_fusion), kind=kCustom, calls=%fused_computation.2 | custom fusion | bytes 8404992 | tf_op jit(solution)/shard_map/gather | solution.py:45
  427.5 26.1 %scatter_custom_fusion.2 = f32[512,256]{1,0:T(8,128)} fusion(s32[4096]{0:T(1024)S(1)} %bitcast.58, f32[4096]{0:T(1024)S(1)} %fusion.59, f32[]{:T(128)} %constant.11.clone.1, bf16[4096,256]{1,0:T(8,128)(2,1)S(1)} %gather_fusion, pred[4096]{0:T(1024)(128)(4,1)S(1)} %compare_and_fusion), kind=kCustom, calls=%fused_computation.39 | custom fusion | flops 4194304 | bytes 2641924 | tf_op jit(solution)/shard_map/scatter-add | solution.py:46
  453.7 85.3 %all-reduce.17.cloned.1.call-done = f32[512,256]{1,0:T(8,128)} async-done(((f32[512,256]{1,0:T(8,128)}), f32[512,256]{1,0:T(8,128)}) %all-reduce.17.cloned.1.call-update) | async-done | bytes 524304 | tf_op jit(solution)/shard_map/psum | solution.py:54
  562.5 26.5 %scatter_custom_fusion.3 = f32[512,256]{1,0:T(8,128)} fusion(s32[4096]{0:T(1024)S(1)} %bitcast.59, f32[4096]{0:T(1024)S(1)} %fusion.58, f32[]{:T(128)} %constant.11.clone.1, bf16[4096,256]{1,0:T(8,128)(2,1)} %copy-done.1, pred[4096]{0:T(1024)(128)(4,1)S(1)} %compare_and_fusion), kind=kCustom, calls=%fused_computation.41 | custom fusion | flops 4194304 | bytes 2641924 | tf_op jit(solution)/shard_map/scatter-add | solution.py:46
  589.6 84.6 %all-reduce.19.cloned.1.call-done = f32[512,256]{1,0:T(8,128)} async-done(((f32[512,256]{1,0:T(8,128)}), f32[512,256]{1,0:T(8,128)}) %all-reduce.19.cloned.1.call-update) | async-done | bytes 524304 | tf_op jit(solution)/shard_map/psum | solution.py:54
  696.4 26.1 %scatter_custom_fusion.4 = f32[512,256]{1,0:T(8,128)} fusion(s32[4096]{0:T(1024)S(1)} %bitcast.60, f32[4096]{0:T(1024)S(1)} %fusion.57, f32[]{:T(128)} %constant.11.clone.1, bf16[4096,256]{1,0:T(8,128)(2,1)S(1)} %copy-done.2, pred[4096]{0:T(1024)(128)(4,1)S(1)} %compare_and_fusion), kind=kCustom, calls=%fused_computation.43 | custom fusion | flops 4194304 | bytes 2641924 | tf_op jit(solution)/shard_map/scatter-add | solution.py:46
  722.6 85.2 %all-reduce.21.cloned.1.call-done = f32[512,256]{1,0:T(8,128)} async-done(((f32[512,256]{1,0:T(8,128)}), f32[512,256]{1,0:T(8,128)}) %all-reduce.21.cloned.1.call-update) | async-done | bytes 524304 | tf_op jit(solution)/shard_map/psum | solution.py:54
  810.7 16.1 %gather_fusion.5 = f32[4096,256]{1,0:T(8,128)} fusion(f32[512,256]{1,0:T(8,128)S(1)} %multiply_add_fusion.3, s32[4096]{0:T(1024)S(1)} %broadcast_clamp_fusion), kind=kCustom, calls=%fused_computation.5 | custom fusion | bytes 8404992 | tf_op jit(solution)/shard_map/gather | solution.py:45
  829.7 26.1 %scatter_custom_fusion.5 = f32[512,256]{1,0:T(8,128)} fusion(s32[4096]{0:T(1024)S(1)} %bitcast.61, f32[4096]{0:T(1024)S(1)} %fusion.56, f32[]{:T(128)} %constant.11.clone.1, bf16[4096,256]{1,0:T(8,128)(2,1)S(1)} %copy-done.2, pred[4096]{0:T(1024)(128)(4,1)S(1)} %compare_and_fusion), kind=kCustom, calls=%fused_computation.45 | custom fusion | flops 4194304 | bytes 2641924 | tf_op jit(solution)/shard_map/scatter-add | solution.py:46
  856.1 85.1 %all-reduce.23.cloned.1.call-done = f32[512,256]{1,0:T(8,128)} async-done(((f32[512,256]{1,0:T(8,128)}), f32[512,256]{1,0:T(8,128)}) %all-reduce.23.cloned.1.call-update) | async-done | bytes 524304 | tf_op jit(solution)/shard_map/psum | solution.py:54
  963.9 26.5 %scatter_custom_fusion.6 = f32[512,256]{1,0:T(8,128)} fusion(s32[4096]{0:T(1024)S(1)} %bitcast.62, f32[4096]{0:T(1024)S(1)} %fusion.55, f32[]{:T(128)} %constant.11.clone.1, bf16[4096,256]{1,0:T(8,128)(2,1)} %copy-done.1, pred[4096]{0:T(1024)(128)(4,1)S(1)} %compare_and_fusion), kind=kCustom, calls=%fused_computation.47 | custom fusion | flops 4194304 | bytes 2641924 | tf_op jit(solution)/shard_map/scatter-add | solution.py:46
  990.5 85.2 %all-reduce.25.cloned.1.call-done = f32[512,256]{1,0:T(8,128)} async-done(((f32[512,256]{1,0:T(8,128)}), f32[512,256]{1,0:T(8,128)}) %all-reduce.25.cloned.1.call-update) | async-done | bytes 524304 | tf_op jit(solution)/shard_map/psum | solution.py:54
  1077.9 16.1 %gather_fusion.7 = f32[4096,256]{1,0:T(8,128)} fusion(f32[512,256]{1,0:T(8,128)S(1)} %multiply_add_fusion.1, s32[4096]{0:T(1024)S(1)} %broadcast_clamp_fusion), kind=kCustom, calls=%fused_computation.7 | custom fusion | bytes 8404992 | tf_op jit(solution)/shard_map/gather | solution.py:45
  1097.5 26.5 %scatter_custom_fusion.7 = f32[512,256]{1,0:T(8,128)} fusion(s32[4096]{0:T(1024)S(1)} %bitcast.63, f32[4096]{0:T(1024)S(1)} %fusion.54, f32[]{:T(128)} %constant.11.clone.1, bf16[4096,256]{1,0:T(8,128)(2,1)} %copy-done.1, pred[4096]{0:T(1024)(128)(4,1)S(1)} %compare_and_fusion), kind=kCustom, calls=%fused_computation.49 | custom fusion | flops 4194304 | bytes 2641924 | tf_op jit(solution)/shard_map/scatter-add | solution.py:46
  1124.3 85.0 %all-reduce.27.cloned.1.call-done = f32[512,256]{1,0:T(8,128)} async-done(((f32[512,256]{1,0:T(8,128)}), f32[512,256]{1,0:T(8,128)}) %all-reduce.27.cloned.1.call-update) | async-done | bytes 524304 | tf_op jit(solution)/shard_map/psum | solution.py:54
  1231.0 26.5 %scatter_custom_fusion.8 = f32[512,256]{1,0:T(8,128)} fusion(s32[4096]{0:T(1024)S(1)} %bitcast.64, f32[4096]{0:T(1024)S(1)} %fusion.53, f32[]{:T(128)} %constant.11.clone.1, bf16[4096,256]{1,0:T(8,128)(2,1)} %copy-done.1, pred[4096]{0:T(1024)(128)(4,1)S(1)} %compare_and_fusion), kind=kCustom, calls=%fused_computation.51 | custom fusion | flops 4194304 | bytes 2641924 | tf_op jit(solution)/shard_map/scatter-add | solution.py:46
  1257.8 85.0 %all-reduce.29.cloned.1.call-done = f32[512,256]{1,0:T(8,128)} async-done(((f32[512,256]{1,0:T(8,128)}), f32[512,256]{1,0:T(8,128)}) %all-reduce.29.cloned.1.call-update) | async-done | bytes 524304 | tf_op jit(solution)/shard_map/psum | solution.py:54
  (115 shorter events, 135.3 us)
Async XLA Ops:
  7.2 37.1 %all-gather.3.cloned.1.call-start = ((), (), s32[]{:S(2)}) async-start(), calls=%async_computation.10 | async-start | bytes 4718592 | tf_op jit(solution)/shard_map/all_gather | solution.py:30
  7.9 164.2 %all-reduce.11.cloned.1.call-start = ((), (), s32[]{:S(2)}) async-start(), calls=%async_computation | async-start | bytes 1048576 | tf_op jit(solution)/shard_map/psum | solution.py:51
  44.3 15.8 %copy-start.10 = (s32[1,1,4096]{2,1,0:T(1,128)S(1)}, s32[1,1,4096]{2,1,0:T(1,128)}, u32[]{:S(2)}) copy-start(s32[1,1,4096]{2,1,0:T(1,128)} %param.7) | copy-start | bytes 49156
  44.3 42.0 %copy-start.9 = (bf16[1,1024,256]{2,1,0:T(8,128)(2,1)S(1)}, bf16[1,1024,256]{2,1,0:T(8,128)(2,1)}, u32[]{:S(2)}) copy-start(bf16[1,1024,256]{2,1,0:T(8,128)(2,1)} %param.5) | copy-start | bytes 1572868
  60.1 367.5 %copy-start.1 = (bf16[4096,256]{1,0:T(8,128)(2,1)}, bf16[4096,256]{1,0:T(8,128)(2,1)S(1)}, u32[]{:S(2)}) copy-start(bf16[4096,256]{1,0:T(8,128)(2,1)S(1)} %gather_fusion) | copy-start | bytes 6291460
  86.2 233.2 %all-reduce.15.cloned.1.call-start = ((), (), s32[]{:S(2)}) async-start(), calls=%async_computation.2 | async-start | bytes 524288 | tf_op jit(solution)/shard_map/psum | solution.py:33
  87.3 318.2 %all-reduce.13.cloned.1.call-start = ((), (), s32[]{:S(2)}) async-start(), calls=%async_computation.1 | async-start | bytes 1048576 | tf_op jit(solution)/shard_map/psum | solution.py:54
  189.2 3.0 copy-start.8
  189.2 216.4 %copy-start = (f32[512,256]{1,0:T(8,128)S(1)}, f32[512,256]{1,0:T(8,128)}, u32[]{:S(2)}) copy-start(f32[512,256]{1,0:T(8,128)} %all-reduce.11.cloned.1.call-done) | copy-start | bytes 1572868
  218.4 320.6 %all-reduce.17.cloned.1.call-start = ((), (), s32[]{:S(2)}) async-start(), calls=%async_computation.3 | async-start | bytes 1048576 | tf_op jit(solution)/shard_map/psum | solution.py:54
  407.4 0.8 copy-start.4
  424.5 114.5 %copy-start.3 = (f32[256,256]{1,0:T(8,128)S(1)}, f32[256,256]{1,0:T(8,128)}, u32[]{:S(2)}) copy-start(f32[256,256]{1,0:T(8,128)} %all-reduce.15.cloned.1.call-done) | copy-start | bytes 786436
  453.6 220.6 %all-reduce.19.cloned.1.call-start = ((), (), s32[]{:S(2)}) async-start(), calls=%async_computation.4 | async-start | bytes 1048576 | tf_op jit(solution)/shard_map/psum | solution.py:54
  589.0 218.8 %all-reduce.21.cloned.1.call-start = ((), (), s32[]{:S(2)}) async-start(), calls=%async_computation.5 | async-start | bytes 1048576 | tf_op jit(solution)/shard_map/psum | solution.py:54
  676.2 1.0 copy-start.6
  677.3 16.1 %copy-start.2 = (bf16[4096,256]{1,0:T(8,128)(2,1)S(1)}, bf16[4096,256]{1,0:T(8,128)(2,1)}, u32[]{:S(2)}) copy-start(bf16[4096,256]{1,0:T(8,128)(2,1)} %copy-done.1) | copy-start | bytes 6291460
  693.3 116.2 %copy-start.7 = (f32[512,256]{1,0:T(8,128)S(1)}, f32[512,256]{1,0:T(8,128)}, u32[]{:S(2)}) copy-start(f32[512,256]{1,0:T(8,128)} %copy-done.6) | copy-start | bytes 1572868
  722.5 218.7 %all-reduce.23.cloned.1.call-start = ((), (), s32[]{:S(2)}) async-start(), calls=%async_computation.6 | async-start | bytes 1048576 | tf_op jit(solution)/shard_map/psum | solution.py:54
  809.8 0.8 copy-start.5
  855.9 219.9 %all-reduce.25.cloned.1.call-start = ((), (), s32[]{:S(2)}) async-start(), calls=%async_computation.7 | async-start | bytes 1048576 | tf_op jit(solution)/shard_map/psum | solution.py:54
  990.5 218.8 %all-reduce.27.cloned.1.call-start = ((), (), s32[]{:S(2)}) async-start(), calls=%async_computation.8 | async-start | bytes 1048576 | tf_op jit(solution)/shard_map/psum | solution.py:54
  1124.0 218.8 %all-reduce.29.cloned.1.call-start = ((), (), s32[]{:S(2)}) async-start(), calls=%async_computation.9 | async-start | bytes 1048576 | tf_op jit(solution)/shard_map/psum | solution.py:54
Sparse Core Ops, SparseCore 0:
  9.7 34.5 all-gather.2
  86.3 85.7 all-reduce.10
  176.8 142.5 all-reduce.14
  322.5 83.0 all-reduce.12
  453.8 85.1 all-reduce.16
  589.2 85.0 all-reduce.18
  722.6 85.1 all-reduce.20
  856.0 85.1 all-reduce.22
  990.6 85.1 all-reduce.24
  1124.1 85.1 all-reduce.26
  1257.6 85.1 all-reduce.28
where the time goes:
time: 1360 us; the launch traced here: 1350 us
  waiting for transfers between devices  901 us (66%)
  other arithmetic  273 us (20%)
  local copies, waits for them, and re-layouts  147 us (11%)
  between operations  15.1 us (1%)
  matrix products  14.8 us (1%)
    psum x8, waiting for transfers between devices, image_every(): summed = lax.psum(local_terms(direction), 'ublk')  682 us
    scatter-add x8, other arithmetic, local_terms(): jax.ops.segment_sum(along[:, None] * rows, items, num_segments=column_items)  210 us
    gather x8, local copies, waits for them, and re-layouts, local_terms(): along = jnp.sum(rows * whole_dir[items], axis=1) * weight  130 us
    psum x1, waiting for transfers between devices, body(): gram = lax.psum(own_gram, ('ublk', 'salt'))  101 us
    psum x1, waiting for transfers between devices, body(): rhs = lax.psum(rhs_terms, 'ublk')  84.7 us
    all_gather x1, waiting for transfers between devices, body(): block = lax.all_gather(shard, 'salt', axis=0, tiled=True)  33.5 us
  transfers between devices with their start and end apart: 11, of which 11 were waited for; matrix products, arithmetic and copies ran while one was open for 4% of the time, Pallas kernels for 0%

commit v1 on v0

--- a/solution.py
+++ b/solution.py
@@ -51,7 +51,7 @@
     rhs = lax.psum(rhs_terms, "ublk")
 
     def image_every(direction):
-        summed = lax.psum(local_terms(direction), "ublk")
+        summed = jnp.sum(lax.all_gather(local_terms(direction), "ublk"), axis=0)
         return finish(summed, direction)
 
     solution_all, resid_all = conjugate(rhs, image_every)

time: 1360 us -> 1260 us (0.926)
  waiting for transfers between devices: 901 us -> 774 us
  other arithmetic: 273 us -> 304 us
    psum x8 -> x0, waiting for transfers between devices: 682 us -> none  [image_every(): summed = lax.psum(local_terms(direction), 'ublk')]
    all_gather x0 -> x8, waiting for transfers between devices: none -> 560 us  [image_every(): summed = jnp.sum(lax.all_gather(local_terms(direction), 'ublk'), axis=0)]
    reduce_sum x0 -> x8, other arithmetic: none -> 33.7 us  [image_every(): summed = jnp.sum(lax.all_gather(local_terms(direction), 'ublk'), axis=0)]
  transfers between devices with their start and end apart: 11 -> 11, of which waited for: 11 -> 11; matrix products, arithmetic and copies ran while one was open for 4% -> 1% of each run, Pallas kernels for 0% -> 0%
where the time goes in v1:
time: 1260 us; the launch traced here: 1250 us
  waiting for transfers between devices  774 us (61%)
  other arithmetic  304 us (24%)
  local copies, waits for them, and re-layouts  147 us (12%)
  between operations  16.9 us (1%)
    all_gather x8, waiting for transfers between devices, image_every(): summed = jnp.sum(lax.all_gather(local_terms(direction), 'ublk'), axis=0)  560 us
    scatter-add x8, other arithmetic, local_terms(): jax.ops.segment_sum(along[:, None] * rows, items, num_segments=column_items)  210 us
    gather x8, local copies, waits for them, and re-layouts, local_terms(): along = jnp.sum(rows * whole_dir[items], axis=1) * weight  130 us
    psum x1, waiting for transfers between devices, body(): gram = lax.psum(own_gram, ('ublk', 'salt'))  93.7 us
    psum x1, waiting for transfers between devices, body(): rhs = lax.psum(rhs_terms, 'ublk')  85.8 us
    reduce_sum x8, other arithmetic, image_every(): summed = jnp.sum(lax.all_gather(local_terms(direction), 'ublk'), axis=0)  33.7 us
    all_gather x1, waiting for transfers between devices, body(): block = lax.all_gather(shard, 'salt', axis=0, tiled=True)  33.5 us
    scatter-add x1, other arithmetic, body(): jax.ops.segment_sum(confid[:, None] * rows, items, num_segments=column_it...  26.1 us
  transfers between devices with their start and end apart: 11, of which 11 were waited for; matrix products, arithmetic and copies ran while one was open for 1% of the time, Pallas kernels for 0%

profile of v1, /device:TPU:0, one launch (start us, length us, event | category | flops | bytes accessed | tf_op | source)
XLA Modules:
  0.0 1253.0 jit_solution(13004228726509729796)
XLA Ops:
  11.6 33.5 %all-gather.19.cloned.1.call-done = bf16[1,8192,256]{2,1,0:T(8,128)(2,1)} async-done(((bf16[1,1024,256]{2,1,0:T(8,128)(2,1)}), bf16[1,8192,256]{2,1,0:T(8,128)(2,1)}) %all-gather.19.cloned.1.call-update) | async-done | bytes 4194320 | tf_op jit(solution)/shard_map/all_gather | solution.py:30
  60.9 26.1 %scatter_custom_fusion = f32[512,256]{1,0:T(8,128)} fusion(s32[4096]{0:T(1024)S(1)} %bitcast.72, f32[4096]{0:T(1024)S(1)} %add_select_fusion, f32[]{:T(128)} %constant.11.clone.1, bf16[4096,256]{1,0:T(8,128)(2,1)S(1)} %gather_fusion, pred[4096]{0:T(1024)(128)(4,1)S(1)} %compare_and_fusion), kind=kCustom, calls=%fused_computation.35 | custom fusion | flops 4194304 | bytes 2641924 | tf_op jit(solution)/shard_map/scatter-add | solution.py:42
  87.1 85.8 %all-reduce.3.cloned.1.call-done = f32[512,256]{1,0:T(8,128)} async-done(((f32[512,256]{1,0:T(8,128)}), f32[512,256]{1,0:T(8,128)}) %all-reduce.3.cloned.1.call-update) | async-done | bytes 524304 | tf_op jit(solution)/shard_map/psum | solution.py:51
  172.9 17.1 %gather_fusion.1 = f32[4096,256]{1,0:T(8,128)} fusion(f32[512,256]{1,0:T(8,128)} %all-reduce.3.cloned.1.call-done, s32[4096]{0:T(1024)S(1)} %broadcast_clamp_fusion), kind=kCustom, calls=%fused_computation.1 | custom fusion | bytes 8404992 | tf_op jit(solution)/shard_map/gather | solution.py:45
  193.0 26.1 %scatter_custom_fusion.1 = f32[512,256]{1,0:T(8,128)} fusion(s32[4096]{0:T(1024)S(1)} %bitcast.73, f32[4096]{0:T(1024)S(1)} %fusion.60, f32[]{:T(128)} %constant.11.clone.1, bf16[4096,256]{1,0:T(8,128)(2,1)S(1)} %gather_fusion, pred[4096]{0:T(1024)(128)(4,1)S(1)} %compare_and_fusion), kind=kCustom, calls=%fused_computation.37 | custom fusion | flops 4194304 | bytes 2641924 | tf_op jit(solution)/shard_map/scatter-add | solution.py:46
  220.8 68.8 %all-gather.21.cloned.1.call-done = f32[8192,256]{1,0:T(8,128)} async-done(((f32[512,256]{1,0:T(8,128)}), f32[8192,256]{1,0:T(8,128)}) %all-gather.21.cloned.1.call-update) | async-done | bytes 8388624 | tf_op jit(solution)/shard_map/all_gather | solution.py:54
  293.7 93.7 %all-reduce.5.cloned.1.call-done = f32[256,256]{1,0:T(8,128)} async-done(((f32[256,256]{1,0:T(8,128)}), f32[256,256]{1,0:T(8,128)}) %all-reduce.5.cloned.1.call-update) | async-done | bytes 262160 | tf_op jit(solution)/shard_map/psum | solution.py:33
  390.2 16.1 %gather_fusion.2 = f32[4096,256]{1,0:T(8,128)} fusion(f32[512,256]{1,0:T(8,128)S(1)} %multiply_add_fusion.7, s32[4096]{0:T(1024)S(1)} %broadcast_clamp_fusion), kind=kCustom, calls=%fused_computation.2 | custom fusion | bytes 8404992 | tf_op jit(solution)/shard_map/gather | solution.py:45
  409.2 26.1 %scatter_custom_fusion.2 = f32[512,256]{1,0:T(8,128)} fusion(s32[4096]{0:T(1024)S(1)} %bitcast.74, f32[4096]{0:T(1024)S(1)} %fusion.59, f32[]{:T(128)} %constant.11.clone.1, bf16[4096,256]{1,0:T(8,128)(2,1)S(1)} %gather_fusion, pred[4096]{0:T(1024)(128)(4,1)S(1)} %compare_and_fusion), kind=kCustom, calls=%fused_computation.39 | custom fusion | flops 4194304 | bytes 2641924 | tf_op jit(solution)/shard_map/scatter-add | solution.py:46
  435.4 68.2 %all-gather.23.cloned.1.call-done = f32[8192,256]{1,0:T(8,128)} async-done(((f32[512,256]{1,0:T(8,128)}), f32[8192,256]{1,0:T(8,128)}) %all-gather.23.cloned.1.call-update) | async-done | bytes 8388624 | tf_op jit(solution)/shard_map/all_gather | solution.py:54
  509.6 16.1 %gather_fusion.3 = f32[4096,256]{1,0:T(8,128)} fusion(f32[512,256]{1,0:T(8,128)S(1)} %multiply_add_fusion.5, s32[4096]{0:T(1024)S(1)} %broadcast_clamp_fusion), kind=kCustom, calls=%fused_computation.3 | custom fusion | bytes 8404992 | tf_op jit(solution)/shard_map/gather | solution.py:45
  529.1 26.5 %scatter_custom_fusion.3 = f32[512,256]{1,0:T(8,128)} fusion(s32[4096]{0:T(1024)S(1)} %bitcast.75, f32[4096]{0:T(1024)S(1)} %fusion.58, f32[]{:T(128)} %constant.11.clone.1, bf16[4096,256]{1,0:T(8,128)(2,1)} %copy-done.1, pred[4096]{0:T(1024)(128)(4,1)S(1)} %compare_and_fusion), kind=kCustom, calls=%fused_computation.41 | custom fusion | flops 4194304 | bytes 2641924 | tf_op jit(solution)/shard_map/scatter-add | solution.py:46
  555.9 70.4 %all-gather.25.cloned.1.call-done = f32[8192,256]{1,0:T(8,128)} async-done(((f32[512,256]{1,0:T(8,128)}), f32[8192,256]{1,0:T(8,128)}) %all-gather.25.cloned.1.call-update) | async-done | bytes 8388624 | tf_op jit(solution)/shard_map/all_gather | solution.py:54
  651.3 26.1 %scatter_custom_fusion.4 = f32[512,256]{1,0:T(8,128)} fusion(s32[4096]{0:T(1024)S(1)} %bitcast.76, f32[4096]{0:T(1024)S(1)} %fusion.57, f32[]{:T(128)} %constant.11.clone.1, bf16[4096,256]{1,0:T(8,128)(2,1)S(1)} %copy-done.2, pred[4096]{0:T(1024)(128)(4,1)S(1)} %compare_and_fusion), kind=kCustom, calls=%fused_computation.43 | custom fusion | flops 4194304 | bytes 2641924 | tf_op jit(solution)/shard_map/scatter-add | solution.py:46
  677.5 70.6 %all-gather.27.cloned.1.call-done = f32[8192,256]{1,0:T(8,128)} async-done(((f32[512,256]{1,0:T(8,128)}), f32[8192,256]{1,0:T(8,128)}) %all-gather.27.cloned.1.call-update) | async-done | bytes 8388624 | tf_op jit(solution)/shard_map/all_gather | solution.py:54
  774.9 26.1 %scatter_custom_fusion.5 = f32[512,256]{1,0:T(8,128)} fusion(s32[4096]{0:T(1024)S(1)} %bitcast.77, f32[4096]{0:T(1024)S(1)} %fusion.56, f32[]{:T(128)} %constant.11.clone.1, bf16[4096,256]{1,0:T(8,128)(2,1)S(1)} %copy-done.2, pred[4096]{0:T(1024)(128)(4,1)S(1)} %compare_and_fusion), kind=kCustom, calls=%fused_computation.45 | custom fusion | flops 4194304 | bytes 2641924 | tf_op jit(solution)/shard_map/scatter-add | solution.py:46
  801.3 70.4 %all-gather.29.cloned.1.call-done = f32[8192,256]{1,0:T(8,128)} async-done(((f32[512,256]{1,0:T(8,128)}), f32[8192,256]{1,0:T(8,128)}) %all-gather.29.cloned.1.call-update) | async-done | bytes 8388624 | tf_op jit(solution)/shard_map/all_gather | solution.py:54
  876.8 16.1 %gather_fusion.6 = f32[4096,256]{1,0:T(8,128)} fusion(f32[512,256]{1,0:T(8,128)S(1)} %multiply_add_fusion.2, s32[4096]{0:T(1024)S(1)} %broadcast_clamp_fusion), kind=kCustom, calls=%fused_computation.6 | custom fusion | bytes 8404992 | tf_op jit(solution)/shard_map/gather | solution.py:45
  896.4 26.5 %scatter_custom_fusion.6 = f32[512,256]{1,0:T(8,128)} fusion(s32[4096]{0:T(1024)S(1)} %bitcast.78, f32[4096]{0:T(1024)S(1)} %fusion.55, f32[]{:T(128)} %constant.11.clone.1, bf16[4096,256]{1,0:T(8,128)(2,1)} %copy-done.1, pred[4096]{0:T(1024)(128)(4,1)S(1)} %compare_and_fusion), kind=kCustom, calls=%fused_computation.47 | custom fusion | flops 4194304 | bytes 2641924 | tf_op jit(solution)/shard_map/scatter-add | solution.py:46
  923.0 70.6 %all-gather.31.cloned.1.call-done = f32[8192,256]{1,0:T(8,128)} async-done(((f32[512,256]{1,0:T(8,128)}), f32[8192,256]{1,0:T(8,128)}) %all-gather.31.cloned.1.call-update) | async-done | bytes 8388624 | tf_op jit(solution)/shard_map/all_gather | solution.py:54
  1018.2 26.5 %scatter_custom_fusion.7 = f32[512,256]{1,0:T(8,128)} fusion(s32[4096]{0:T(1024)S(1)} %bitcast.79, f32[4096]{0:T(1024)S(1)} %fusion.54, f32[]{:T(128)} %constant.11.clone.1, bf16[4096,256]{1,0:T(8,128)(2,1)} %copy-done.1, pred[4096]{0:T(1024)(128)(4,1)S(1)} %compare_and_fusion), kind=kCustom, calls=%fused_computation.49 | custom fusion | flops 4194304 | bytes 2641924 | tf_op jit(solution)/shard_map/scatter-add | solution.py:46
  1045.0 70.4 %all-gather.33.cloned.1.call-done = f32[8192,256]{1,0:T(8,128)} async-done(((f32[512,256]{1,0:T(8,128)}), f32[8192,256]{1,0:T(8,128)}) %all-gather.33.cloned.1.call-update) | async-done | bytes 8388624 | tf_op jit(solution)/shard_map/all_gather | solution.py:54
  1140.0 26.5 %scatter_custom_fusion.8 = f32[512,256]{1,0:T(8,128)} fusion(s32[4096]{0:T(1024)S(1)} %bitcast.80, f32[4096]{0:T(1024)S(1)} %fusion.53, f32[]{:T(128)} %constant.11.clone.1, bf16[4096,256]{1,0:T(8,128)(2,1)} %copy-done.1, pred[4096]{0:T(1024)(128)(4,1)S(1)} %compare_and_fusion), kind=kCustom, calls=%fused_computation.51 | custom fusion | flops 4194304 | bytes 2641924 | tf_op jit(solution)/shard_map/scatter-add | solution.py:46
  1166.9 70.4 %all-gather.35.cloned.1.call-done = f32[8192,256]{1,0:T(8,128)} async-done(((f32[512,256]{1,0:T(8,128)}), f32[8192,256]{1,0:T(8,128)}) %all-gather.35.cloned.1.call-update) | async-done | bytes 8388624 | tf_op jit(solution)/shard_map/all_gather | solution.py:54
  (127 shorter events, 161.4 us)
Async XLA Ops:
  8.0 37.1 %all-gather.19.cloned.1.call-start = ((), (), s32[]{:S(2)}) async-start(), calls=%async_computation.2 | async-start | bytes 4718592 | tf_op jit(solution)/shard_map/all_gather | solution.py:30
  8.7 164.1 %all-reduce.3.cloned.1.call-start = ((), (), s32[]{:S(2)}) async-start(), calls=%async_computation | async-start | bytes 1048576 | tf_op jit(solution)/shard_map/psum | solution.py:51
  45.1 15.8 %copy-start.12 = (s32[1,1,4096]{2,1,0:T(1,128)S(1)}, s32[1,1,4096]{2,1,0:T(1,128)}, u32[]{:S(2)}) copy-start(s32[1,1,4096]{2,1,0:T(1,128)} %param.7) | copy-start | bytes 49156
  60.8 348.4 %copy-start.1 = (bf16[4096,256]{1,0:T(8,128)(2,1)}, bf16[4096,256]{1,0:T(8,128)(2,1)S(1)}, u32[]{:S(2)}) copy-start(bf16[4096,256]{1,0:T(8,128)(2,1)S(1)} %gather_fusion) | copy-start | bytes 6291460
  87.0 202.7 %all-gather.21.cloned.1.call-start = ((), (), s32[]{:S(2)}) async-start(), calls=%async_computation.3 | async-start | bytes 8912896 | tf_op jit(solution)/shard_map/all_gather | solution.py:54
  190.0 3.0 copy-start.10
  190.0 29.2 %copy-start.11 = (bf16[1,1024,256]{2,1,0:T(8,128)(2,1)S(1)}, bf16[1,1024,256]{2,1,0:T(8,128)(2,1)}, u32[]{:S(2)}) copy-start(bf16[1,1024,256]{2,1,0:T(8,128)(2,1)} %param.5) | copy-start | bytes 1572868
  219.2 168.3 %all-reduce.5.cloned.1.call-start = ((), (), s32[]{:S(2)}) async-start(), calls=%async_computation.1 | async-start | bytes 524288 | tf_op jit(solution)/shard_map/psum | solution.py:33
  220.3 283.4 %all-gather.23.cloned.1.call-start = ((), (), s32[]{:S(2)}) async-start(), calls=%async_computation.4 | async-start | bytes 8912896 | tf_op jit(solution)/shard_map/all_gather | solution.py:54
  289.7 97.8 %copy-start = (f32[512,256]{1,0:T(8,128)S(1)}, f32[512,256]{1,0:T(8,128)}, u32[]{:S(2)}) copy-start(f32[512,256]{1,0:T(8,128)} %all-reduce.3.cloned.1.call-done) | copy-start | bytes 1572868
  389.1 0.8 copy-start.4
  435.4 191.0 %all-gather.25.cloned.1.call-start = ((), (), s32[]{:S(2)}) async-start(), calls=%async_computation.5 | async-start | bytes 8912896 | tf_op jit(solution)/shard_map/all_gather | solution.py:54
  503.6 4.1 copy-start.3
  503.6 4.7 copy-start.5
  555.7 192.5 %all-gather.27.cloned.1.call-start = ((), (), s32[]{:S(2)}) async-start(), calls=%async_computation.6 | async-start | bytes 8912896 | tf_op jit(solution)/shard_map/all_gather | solution.py:54
  631.3 1.0 copy-start.8
  632.3 16.1 %copy-start.2 = (bf16[4096,256]{1,0:T(8,128)(2,1)S(1)}, bf16[4096,256]{1,0:T(8,128)(2,1)}, u32[]{:S(2)}) copy-start(bf16[4096,256]{1,0:T(8,128)(2,1)} %copy-done.1) | copy-start | bytes 6291460
  677.5 194.2 %all-gather.29.cloned.1.call-start = ((), (), s32[]{:S(2)}) async-start(), calls=%async_computation.7 | async-start | bytes 8912896 | tf_op jit(solution)/shard_map/all_gather | solution.py:54
  748.1 6.6 copy-start.9
  754.9 0.8 copy-start.6
  801.1 192.5 %all-gather.31.cloned.1.call-start = ((), (), s32[]{:S(2)}) async-start(), calls=%async_computation.8 | async-start | bytes 8912896 | tf_op jit(solution)/shard_map/all_gather | solution.py:54
  871.7 4.7 copy-start.7
  922.9 192.5 %all-gather.33.cloned.1.call-start = ((), (), s32[]{:S(2)}) async-start(), calls=%async_computation.9 | async-start | bytes 8912896 | tf_op jit(solution)/shard_map/all_gather | solution.py:54
  1044.7 192.5 %all-gather.35.cloned.1.call-start = ((), (), s32[]{:S(2)}) async-start(), calls=%async_computation.10 | async-start | bytes 8912896 | tf_op jit(solution)/shard_map/all_gather | solution.py:54
Sparse Core Ops, SparseCore 0:
  10.5 34.5 all-gather.18
  87.1 85.7 all-reduce.2
  219.3 70.3 all-gather.20
  435.5 68.1 all-gather.22
  555.8 70.4 all-gather.24
  677.6 70.4 all-gather.26
  801.2 70.4 all-gather.28
  923.0 70.4 all-gather.30
  1044.9 70.4 all-gather.32
  1166.7 70.4 all-gather.34
Sparse Core Ops, SparseCore 1:
  224.4 163.0 all-reduce.4
